TPU v7x, 128 devices: a whole 4x4x4 slice. The times are simulated.
128 devices in a mesh: slot: 16 (over y, z), head: 2 (over x_lo), conv: 4 (over x_hi, core).
Axes of the slice: x: 4 (x_hi: 2, x_lo: 2; x = x_hi * 2 + x_lo), y: 4, z: 4, core: 2. Of those that a mesh axis runs over, the one named last changes fastest.
Arguments:
- queries: bfloat16 [1024, 64, 128], P(('conv', 'slot'), 'head'), may hold values from -96 to 96
- out_grad: bfloat16 [1024, 64, 128], P(('conv', 'slot'), 'head'), may hold values from -768 to 768
- row_positions: int32 [1024], P('conv'), may hold values from 0 to 8191
- slot_offsets: int32 [16384], P('slot'), may hold values from 0 to 16382, as said below
- cache: float32 [2, 16384, 4, 128], P(None, 'slot', 'head'), may hold values from -12 to 12
- first_moment: float32 [2, 16384, 4, 128], P(None, 'slot', 'head'), may hold values from -6 to 6
- second_moment: float32 [2, 16384, 4, 128], P(None, 'slot', 'head'), may hold values from 0.01 to 1000
Outputs:
- new_cache: float32 [2, 16384, 4, 128], P(None, 'slot', 'head')
- new_first_moment: float32 [2, 16384, 4, 128], P(None, 'slot', 'head')
- new_second_moment: float32 [2, 16384, 4, 128], P(None, 'slot', 'head')
- query_grad: float32 [1024, 64, 128], P(('conv', 'slot'), 'head')
Inputs may be any that keep to these rules, and one draw needn't show every extreme that they name: `slot_offsets`: never falls from one slot to the next; its first two entries are 0.
All inputs are finite; a program needn't handle non-finite values.
Results may differ from a plain program's by a relative error of at most 0.012.
The roundings to bfloat16 on the way count: a program that leaves them out, or rounds other values in their place, can miss the bound.
Values may be sent and summed in bfloat16 or wider, within the bound.
A program may use at most 128 MiB of HBM per device.

v0:
```python
import math
import jax
import jax.numpy as jnp
from jax import lax
from jax.sharding import PartitionSpec as P

STEP = 20
learn_rate = 0.01
beta_one = 0.9
beta_two = 0.95
adam_eps = 1e-08
masked_score = -1e30


def merged(x, axis, combine):
    everything = jax.tree.map(lambda part: lax.all_gather(part, axis), x)
    leading = jax.tree.map(lambda part: part[0], everything)

    def lap(k, so_far):
        return combine(so_far, jax.tree.map(lambda part: part[k], everything))

    return lax.fori_loop(1, lax.axis_size(axis), lap, leading)


def merge_pairs(earlier, later):
    largest = jnp.maximum(earlier[0], later[0])
    return (
        largest,
        earlier[1] * jnp.exp(earlier[0] - largest) + later[1] * jnp.exp(later[0] - largest),
    )


def local(queries, out_grad, row_positions, slot_offsets, cache, first_moment, second_moment):
    query_all, grad_all = (
        lax.all_gather(queries, "slot", axis=0, tiled=True),
        lax.all_gather(out_grad, "slot", axis=0, tiled=True),
    )
    total_rows, head_count, head_width = query_all.shape
    kv_count = cache.shape[2]
    group_heads = head_count // kv_count
    score_scale = 1.0 / math.sqrt(head_width)
    block_rows = min(64, total_rows)
    block_count = total_rows // block_rows
    key_half = cache[0].astype(jnp.bfloat16)
    value_half = cache[1].astype(jnp.bfloat16)
    query_blocks = query_all.reshape(block_count, block_rows, kv_count, group_heads, head_width)
    grad_blocks = grad_all.reshape(block_count, block_rows, kv_count, group_heads, head_width)
    visible_all = (slot_offsets[None, :] <= row_positions[:, None]).reshape(
        block_count, block_rows, -1
    )

    def masked_scores(query_block, visible):
        raw_score = (
            jnp.einsum("rkgd,skd->rkgs", query_block, key_half, preferred_element_type=jnp.float32)
            * score_scale
        )
        return jnp.where(visible[:, None, None, :], raw_score, masked_score)

    def weights_from(scores, visible, offset):
        return jnp.where(visible[:, None, None, :], jnp.exp(scores - offset[..., None]), 0.0)

    def gradient_products(grad_block):
        return jnp.einsum(
            "rkgd,skd->rkgs", grad_block, value_half, preferred_element_type=jnp.float32
        )

    def max_pass(inputs):
        query_block, visible = inputs
        scores = masked_scores(query_block, visible)
        largest = jnp.max(scores, axis=-1)
        return (largest, jnp.sum(weights_from(scores, visible, largest), axis=-1))

    largest, denominator = lax.map(max_pass, (query_blocks, visible_all))
    largest, denominator = merged((largest, denominator), "slot", merge_pairs)
    log_total = largest + jnp.log(denominator)

    def product_pass(inputs):
        query_block, grad_block, visible, block_total = inputs
        probability = weights_from(masked_scores(query_block, visible), visible, block_total)
        return jnp.sum(probability * gradient_products(grad_block), axis=-1)

    partial_sum = lax.map(product_pass, (query_blocks, grad_blocks, visible_all, log_total))
    row_sum = lax.psum(partial_sum, "slot")

    def last_pass(running, inputs):
        key_grad, value_grad = running
        query_block, grad_block, visible, block_total, block_sum = inputs
        probability = weights_from(masked_scores(query_block, visible), visible, block_total)
        prob_grad = gradient_products(grad_block)
        score_grad = (probability * (prob_grad - block_sum[..., None])).astype(jnp.bfloat16)
        prob_half = probability.astype(jnp.bfloat16)
        value_grad = value_grad + jnp.einsum(
            "rkgs,rkgd->skd", prob_half, grad_block, preferred_element_type=jnp.float32
        )
        key_grad = (
            key_grad
            + jnp.einsum(
                "rkgs,rkgd->skd", score_grad, query_block, preferred_element_type=jnp.float32
            )
            * score_scale
        )
        query_part = (
            jnp.einsum("rkgs,skd->rkgd", score_grad, key_half, preferred_element_type=jnp.float32)
            * score_scale
        )
        return ((key_grad, value_grad), query_part)

    empty_grad = jnp.zeros(key_half.shape, jnp.float32)
    (key_grad, value_grad), query_parts = lax.scan(
        last_pass,
        (empty_grad, empty_grad),
        (query_blocks, grad_blocks, visible_all, log_total, row_sum),
    )
    query_terms = query_parts.reshape(total_rows, head_count, head_width)
    summed = lax.psum(query_terms, "slot")
    own_rows = queries.shape[0]
    query_grad = lax.dynamic_slice_in_dim(summed, lax.axis_index("slot") * own_rows, own_rows, 0)
    key_total, value_total = lax.psum((key_grad, value_grad), "conv")
    slot_grad = jnp.stack([key_total, value_total])
    new_first = beta_one * first_moment + (1.0 - beta_one) * slot_grad
    new_second = beta_two * second_moment + (1.0 - beta_two) * slot_grad * slot_grad
    first_fix = 1.0 - beta_one**STEP
    second_fix = 1.0 - beta_two**STEP
    new_cache = cache - learn_rate * (new_first / first_fix) / (
        jnp.sqrt(new_second / second_fix) + adam_eps
    )
    return (new_cache, new_first, new_second, query_grad)


def solution(mesh):
    in_specs = (
        P(("conv", "slot"), "head", None),
        P(("conv", "slot"), "head", None),
        P("conv"),
        P("slot"),
        P(None, "slot", "head", None),
        P(None, "slot", "head", None),
        P(None, "slot", "head", None),
    )
    out_specs = (
        P(None, "slot", "head", None),
        P(None, "slot", "head", None),
        P(None, "slot", "head", None),
        P(("conv", "slot"), "head", None),
    )
    return jax.shard_map(local, mesh=mesh, in_specs=in_specs, out_specs=out_specs, check_vma=False)
```

profile of v0, /device:TPU:1, one launch (start us, length us, event | category | flops | bytes accessed | tf_op | source)
XLA Modules:
  0.0 525.3 jit_solution(10511550598650439508)
XLA Ops:
  9.5 1.8 copy.70
  13.1 43.8 %all-gather.5.cloned.1.call-done = bf16[256,32,128]{2,1,0:T(8,128)(2,1)} async-done(((bf16[16,32,128]{2,1,0:T(8,128)(2,1)}), bf16[256,32,128]{2,1,0:T(8,128)(2,1)}) %all-gather.5.cloned.1.call-update) | async-done | bytes 2097168 | tf_op jit(solution)/shard_map/all_gather | solution.py:35
  56.9 3.3 copy.50
  60.1 43.2 %all-gather.7.cloned.1.call-done = bf16[256,32,128]{2,1,0:T(8,128)(2,1)} async-done(((bf16[16,32,128]{2,1,0:T(8,128)(2,1)}), bf16[256,32,128]{2,1,0:T(8,128)(2,1)}) %all-gather.7.cloned.1.call-update) | async-done | bytes 2097168 | tf_op jit(solution)/shard_map/all_gather | solution.py:36
  103.3 3.3 copy.51
  106.6 23.2 %while.54 = (s32[]{:T(128)}, f32[4,64,2,16]{1,3,2,0:T(8,128)S(1)}, f32[4,64,2,16]{1,3,2,0:T(8,128)S(1)}, pred[4,64,1024]{2,1,0:T(8,128)(4,1)S(1)}, bf16[4,64,2,1...) while((s32[]{:T(128)}, f32[4,64,2,16]{1,3,2,0:T(8,128)S(1)}, ...), condition=%wide.region_3.4_spmd, body=%wide.region_0.3_spmd.sunk | while | flops 553644032 | bytes 18210912 | solution.py:73
  106.6 2.8 bitcast_reduce_fusion.2
  109.4 2.8 fusion.87
  112.4 2.8 bitcast_reduce_fusion.2
  115.2 2.8 fusion.87
  118.2 2.8 bitcast_reduce_fusion.2
  121.0 2.8 fusion.87
  124.0 2.8 bitcast_reduce_fusion.2
  126.8 2.8 fusion.87
  129.8 19.1 %all-gather.1 = f32[64,64,2,16]{1,3,2,0:T(8,128)S(1)} all-gather(f32[4,64,2,16]{1,3,2,0:T(8,128)S(1)} %get-tuple-element.272), channel_id=3, replica_groups=mesh['slot'=16,'head'=2,'conv'=4] {'slot'}, dimensions={0}, use_global_device_ids=true | all-gather | bytes 557056 | tf_op jit(solution)/shard_map/all_gather | solution.py:16
  148.9 17.4 %all-gather = f32[64,64,2,16]{1,3,2,0:T(8,128)S(1)} all-gather(f32[4,64,2,16]{1,3,2,0:T(8,128)S(1)} %get-tuple-element.271), channel_id=2, replica_groups=mesh['slot'=16,'head'=2,'conv'=4] {'slot'}, dimensions={0}, use_global_device_ids=true | all-gather | bytes 557056 | tf_op jit(solution)/shard_map/all_gather | solution.py:16
  166.3 1.0 copy-done.4
  167.2 13.9 %while.55 = (s32[]{:T(128)}, f32[4,64,2,16]{1,3,2,0:T(8,128)S(1)}, f32[4,64,2,16]{1,3,2,0:T(8,128)S(1)}, f32[16,4,64,2,16]{2,4,3,1,0:T(8,128)}, f32[16,4,64,2,16...) while((s32[]{:T(128)}, f32[4,64,2,16]{1,3,2,0:T(8,128)S(1)}, f32[4,64,2,16]{1,3,2,0:T(8,128)S(1)}, ...), condition=%wide.region_5.6_spmd, body=%wide.region_4.5_spmd.sunk | while | flops 49157 | bytes 196731 | solution.py:22
  168.1 0.9 fusion.88
  169.1 0.9 fusion.88
  170.0 0.9 fusion.88
  181.5 31.2 %while.56 = (s32[]{:T(128)}, f32[4,64,2,16]{3,1,2,0:T(8,128)}, pred[4,64,1024]{2,1,0:T(8,128)(4,1)S(1)}, bf16[4,64,2,16,128]{4,3,1,2,0:T(8,128)(2,1)}, bf16[1024...) while((s32[]{:T(128)}, f32[4,64,2,16]{3,1,2,0:T(8,128)}, ...), condition=%wide.region_8.9_spmd, body=%wide.region_6.8_spmd.sunk | while | flops 1086322688 | bytes 21397652 | solution.py:82
  181.5 2.4 fusion.93
  183.9 4.7 fusion.94
  189.4 2.4 fusion.93
  191.7 4.7 fusion.94
  197.1 2.4 fusion.93
  199.5 4.7 fusion.94
  204.9 2.4 fusion.93
  207.3 4.7 fusion.94
  212.7 61.1 %psum.28 = f32[4,64,2,16]{3,1,2,0:T(8,128)S(1)} all-reduce(f32[4,64,2,16]{3,1,2,0:T(8,128)} %get-tuple-element.275), channel_id=1, replica_groups=mesh['slot'=16,'head'=2,'conv'=4] {'slot'}, use_global_device_ids=true, to_apply=%region_9.10 | all-reduce | flops 8192 | bytes 65536 | tf_op jit(solution)/shard_map/psum | solution.py:83
  273.8 52.7 %while.57 = (s32[]{:T(128)}, f32[1024,2,128]{0,2,1:T(8,128)S(1)}, f32[1024,2,128]{0,2,1:T(8,128)S(1)}, f32[4,64,2,16,128]{4,3,2,1,0:T(8,128)}, bf16[4,64,2,16,12...) while((s32[]{:T(128)}, f32[1024,2,128]{0,2,1:T(8,128)S(1)}, ...), condition=%wide.region_11.12_spmd.clone, body=%wide.region_10.11_spmd.clone.sunk | while | flops 2711093248 | bytes 59867360 | solution.py:109
  273.9 2.4 fusion.105
  276.4 2.7 fusion.108
  279.1 3.5 fusion.106
  282.5 2.1 fusion.107
  284.7 1.2 fusion.109
  285.9 1.1 copy_dynamic-update-slice_fusion.2
  287.1 2.4 fusion.105
  289.6 2.7 fusion.108
  292.2 3.5 fusion.106
  295.7 2.1 fusion.107
  297.8 1.2 fusion.109
  299.1 1.2 copy_dynamic-update-slice_fusion.2
  300.3 2.4 fusion.105
  302.7 2.7 fusion.108
  305.4 3.5 fusion.106
  308.9 2.1 fusion.107
  311.0 1.2 fusion.109
  312.3 1.1 copy_dynamic-update-slice_fusion.2
  313.4 2.4 fusion.105
  315.9 2.7 fusion.108
  318.6 3.5 fusion.106
  322.1 2.1 fusion.107
  324.2 1.2 fusion.109
  325.4 1.1 copy_dynamic-update-slice_fusion.2
  326.6 1.3 copy.52
  327.9 1.3 copy.53
  329.7 81.8 %all-reduce.6.cloned.1.call-done = (f32[1,1024,2,128]{3,2,1,0:T(2,128)}, f32[1,1024,2,128]{3,2,1,0:T(2,128)}) async-done(((f32[1,1024,2,128]{3,2,1,0:T(2,128)}, f32[1,1024,2,128]{3,2,1,0:T(2,128)}), (f32[1,1024,2,128]{3,2,1,0:T(2,128)}, f32[1,1024,2,128]{3,2,1,0:T(2,128)})) %all-reduce.6.cloned.1.call-update) | async-done | bytes 2097168 | tf_op jit(solution)/shard_map/psum | solution.py:118
  411.5 1.4 constant_dynamic-update-slice_fusion.3
  413.0 1.5 constant_dynamic-update-slice_fusion.2
  414.5 8.0 %divide_subtract_fusion = (f32[2,1024,2,128]{3,2,1,0:T(2,128)}, f32[2,1024,2,128]{3,2,1,0:T(2,128)}, f32[2,1024,2,128]{3,2,1,0:T(2,128)}) fusion(f32[2,1024,2,128]{3,2,1,0:T(2,128)S(1)} %copy-done, f32[2,1024,2,128]{3,2,1,0:T(2,128)S(1)} %constant_dynamic-update-slice_fusion.2, f32[2,1024,2,128]{3,2,1,0:T(2,128)S(1)} %copy-done.1, ...), kind=kLoop, calls=%fused_computation.80 | loop fusion | flops 6291456 | bytes 14680064 | tf_op jit(solution)/shard_map/sub | solution.py:124
  422.5 94.6 %all-reduce.4.cloned.1.call-done = f32[256,32,128]{2,1,0:T(8,128)} async-done(((f32[256,32,128]{2,1,0:T(8,128)}), f32[256,32,128]{2,1,0:T(8,128)}) %all-reduce.4.cloned.1.call-update) | async-done | bytes 4194320 | tf_op jit(solution)/shard_map/psum | solution.py:115
  517.1 1.7 constant_dynamic-slice_fusion
  (103 shorter events, 19.2 us)
Async XLA Ops:
  7.2 49.7 %all-gather.5.cloned.1.call-start = ((), (), s32[]{:S(2)}) async-start(), calls=%async_computation | async-start | bytes 2228224 | tf_op jit(solution)/shard_map/all_gather | solution.py:35
  7.9 95.4 %all-gather.7.cloned.1.call-start = ((), (), s32[]{:S(2)}) async-start(), calls=%async_computation.1 | async-start | bytes 2228224 | tf_op jit(solution)/shard_map/all_gather | solution.py:36
  8.6 402.9 %all-reduce.6.cloned.1.call-start = ((), (), s32[]{:S(2)}) async-start(), calls=%async_computation.3 | async-start | bytes 4194304 | tf_op jit(solution)/shard_map/psum | solution.py:118
  166.2 1.0 copy-start.4
  181.4 92.4 %copy-start.5 = (f32[1024,2,128]{0,2,1:T(8,128)S(1)}, f32[1024,2,128]{0,2,1:T(8,128)}, u32[]{:S(2)}) copy-start(f32[1024,2,128]{0,2,1:T(8,128)} %custom-call.1) | copy-start | bytes 3145732
  181.5 2.4 copy-start.6
  189.3 2.4 copy-start.6
  197.1 2.4 copy-start.6
  204.9 2.4 copy-start.6
  273.9 2.5 copy-start.3
  276.4 2.7 copy-start.7
  287.1 2.5 copy-start.3
  289.5 2.7 copy-start.7
  300.3 2.5 copy-start.3
  302.7 2.7 copy-start.7
  313.4 2.5 copy-start.3
  315.9 2.7 copy-start.7
  329.2 187.9 %all-reduce.4.cloned.1.call-start = ((), (), s32[]{:S(2)}) async-start(), calls=%async_computation.2 | async-start | bytes 8388608 | tf_op jit(solution)/shard_map/psum | solution.py:115
  329.2 85.2 %copy-start = (f32[2,1024,2,128]{3,2,1,0:T(2,128)S(1)}, f32[2,1024,2,128]{3,2,1,0:T(2,128)}, u32[]{:S(2)}) copy-start(f32[2,1024,2,128]{3,2,1,0:T(2,128)} %param.19) | copy-start | bytes 6291460
  411.5 3.0 copy-start.1
  411.5 3.0 copy-start.2
Sparse Core Ops, SparseCore 0:
  10.1 46.6 all-gather.4
  59.0 44.2 all-gather.6
  329.3 82.1 all-reduce.5
  414.7 102.2 all-reduce.3
where the time goes:
time: 527 us; the launch traced here: 525 us
  waiting for transfers between devices  265 us (50%)
  blocking collectives  97.6 us (19%)
  matrix products  87.3 us (17%)
  other arithmetic  33.9 us (6%)
  local copies, waits for them, and re-layouts  26.4 us (5%)
  between operations  13.9 us (3%)
    psum x1, waiting for transfers between devices, local(): summed = lax.psum(query_terms, 'slot')  94.6 us
    psum x1, waiting for transfers between devices, local(): key_total, value_total = lax.psum((key_grad, value_grad), 'conv')  81.8 us
    psum x1, blocking collectives, local(): row_sum = lax.psum(partial_sum, 'slot')  61.1 us
    all_gather x1, waiting for transfers between devices, local(): lax.all_gather(queries, 'slot', axis=0, tiled=True)  43.8 us
    all_gather x1, waiting for transfers between devices, local(): lax.all_gather(out_grad, 'slot', axis=0, tiled=True)  43.2 us
    all_gather x2, blocking collectives, merged(): everything = jax.tree.map(lambda part: lax.all_gather(part, axis), x)  36.5 us
    dot_general x8, matrix products, gradient_products(): jnp.einsum('rkgd,skd->rkgs', grad_block, value_half, preferred_element_ty...  32.8 us
    dot_general x12, matrix products, masked_scores(): jnp.einsum('rkgd,skd->rkgs', query_block, key_half, preferred_element_typ...  30.3 us
  transfers between devices with their start and end apart: 4, of which 4 were waited for; matrix products, arithmetic and copies ran while one was open for 4% of the time, Pallas kernels for 0%

commit v1 on v0

--- a/solution.py
+++ b/solution.py
@@ -31,9 +31,17 @@
 
 
 def local(queries, out_grad, row_positions, slot_offsets, cache, first_moment, second_moment):
+
+    def wrap_view(on_dim, across, vals):
+        state_now = jax.lax.axis_size(across)
+        heard = jnp.stack(state_now * [vals], axis=0)
+        v1 = jax.lax.all_to_all(heard, across, 0, 0)
+        side_arr = jnp.concatenate(v1, axis=on_dim)
+        return side_arr
+
     query_all, grad_all = (
         lax.all_gather(queries, "slot", axis=0, tiled=True),
-        lax.all_gather(out_grad, "slot", axis=0, tiled=True),
+        wrap_view(0, "slot", out_grad),
     )
     total_rows, head_count, head_width = query_all.shape
     kv_count = cache.shape[2]

time: 527 us -> 496 us (0.941)
  waiting for transfers between devices: 265 us -> 222 us
  starting transfers between devices: 0.16 us -> 8.89 us
    all_gather x1 -> x0, waiting for transfers between devices: 43.2 us -> none  [local(): lax.all_gather(out_grad, 'slot', axis=0, tiled=True)]
    all_to_all x0 -> x1, waiting for transfers between devices: none -> 27.2 us  [wrap_view(): v1 = jax.lax.all_to_all(heard, across, 0, 0)]
    all_gather x1, waiting for transfers between devices: 43.8 us -> 18.6 us  [local(): lax.all_gather(queries, 'slot', axis=0, tiled=True)]
    all_to_all x0 -> x1, starting transfers between devices: none -> 8.77 us  [wrap_view(): v1 = jax.lax.all_to_all(heard, across, 0, 0)]
    unnamed x14 -> x12, local copies, waits for them, and re-layouts: 10.8 us -> 10.6 us
where the time goes in v1:
time: 496 us; the launch traced here: 494 us
  waiting for transfers between devices  222 us (45%)
  blocking collectives  97.6 us (20%)
  matrix products  87.3 us (18%)
  other arithmetic  35.1 us (7%)
  local copies, waits for them, and re-layouts  28.1 us (6%)
  between operations  13.9 us (3%)
  starting transfers between devices  8.89 us (2%)
    psum x1, waiting for transfers between devices, local(): summed = lax.psum(query_terms, 'slot')  93.3 us
    psum x1, waiting for transfers between devices, local(): key_total, value_total = lax.psum((key_grad, value_grad), 'conv')  81.6 us
    psum x1, blocking collectives, local(): row_sum = lax.psum(partial_sum, 'slot')  61.1 us
    all_gather x2, blocking collectives, merged(): everything = jax.tree.map(lambda part: lax.all_gather(part, axis), x)  36.5 us
    dot_general x8, matrix products, gradient_products(): jnp.einsum('rkgd,skd->rkgs', grad_block, value_half, preferred_element_ty...  32.8 us
    dot_general x12, matrix products, masked_scores(): jnp.einsum('rkgd,skd->rkgs', query_block, key_half, preferred_element_typ...  30.3 us
    all_to_all x1, waiting for transfers between devices, wrap_view(): v1 = jax.lax.all_to_all(heard, across, 0, 0)  27.2 us
    all_gather x1, waiting for transfers between devices, local(): lax.all_gather(queries, 'slot', axis=0, tiled=True)  18.6 us
  transfers between devices with their start and end apart: 4, of which 4 were waited for; matrix products, arithmetic and copies ran while one was open for 4% of the time, Pallas kernels for 0%

profile of v1, /device:TPU:1, one launch (start us, length us, event | category | flops | bytes accessed | tf_op | source)
XLA Modules:
  0.0 493.7 jit_solution(15138083959505312015)
XLA Ops:
  7.9 2.6 stack.8
  10.5 8.8 %all-to-all-start = ((bf16[16,16,32,128]{3,2,1,0:T(8,128)(2,1)}), bf16[16,16,32,128]{3,2,1,0:T(8,128)(2,1)}, u32[]{:S(2)}, u32[]{:S(2)}) async-start(bf16[16,16,32,128]{3,2,1,0:T(8,128)(2,1)} %stack.8), calls=%async_computation | async-start | bytes 4194304 | tf_op jit(solution)/shard_map/all_to_all | solution.py:38
  19.5 1.8 copy.70
  22.4 27.2 %all-to-all-done = bf16[16,16,32,128]{3,2,1,0:T(8,128)(2,1)} async-done(((bf16[16,16,32,128]{3,2,1,0:T(8,128)(2,1)}), bf16[16,16,32,128]{3,2,1,0:T(8,128)(2,1)}, u32[]{:S(2)}, u32[]{:S(2)}) %all-to-all-start) | async-done | bytes 2097184 | tf_op jit(solution)/shard_map/all_to_all | solution.py:38
  49.7 3.3 copy.51
  53.0 18.6 %all-gather.4.cloned.1.call-done = bf16[256,32,128]{2,1,0:T(8,128)(2,1)} async-done(((bf16[16,32,128]{2,1,0:T(8,128)(2,1)}), bf16[256,32,128]{2,1,0:T(8,128)(2,1)}) %all-gather.4.cloned.1.call-update) | async-done | bytes 2097168 | tf_op jit(solution)/shard_map/all_gather | solution.py:43
  71.5 3.3 copy.50
  74.8 23.2 %while.54 = (s32[]{:T(128)}, f32[4,64,2,16]{1,3,2,0:T(8,128)S(1)}, f32[4,64,2,16]{1,3,2,0:T(8,128)S(1)}, pred[4,64,1024]{2,1,0:T(8,128)(4,1)S(1)}, bf16[4,64,2,1...) while((s32[]{:T(128)}, f32[4,64,2,16]{1,3,2,0:T(8,128)S(1)}, ...), condition=%wide.region_3.4_spmd, body=%wide.region_0.3_spmd.sunk | while | flops 553644032 | bytes 18210912 | solution.py:81
  74.8 2.8 bitcast_reduce_fusion.2
  77.6 2.8 fusion.87
  80.6 2.8 bitcast_reduce_fusion.2
  83.4 2.8 fusion.87
  86.4 2.8 bitcast_reduce_fusion.2
  89.2 2.8 fusion.87
  92.2 2.8 bitcast_reduce_fusion.2
  95.0 2.8 fusion.87
  98.0 19.1 %all-gather.1 = f32[64,64,2,16]{1,3,2,0:T(8,128)S(1)} all-gather(f32[4,64,2,16]{1,3,2,0:T(8,128)S(1)} %get-tuple-element.272), channel_id=3, replica_groups=mesh['slot'=16,'head'=2,'conv'=4] {'slot'}, dimensions={0}, use_global_device_ids=true | all-gather | bytes 557056 | tf_op jit(solution)/shard_map/all_gather | solution.py:16
  117.1 17.4 %all-gather = f32[64,64,2,16]{1,3,2,0:T(8,128)S(1)} all-gather(f32[4,64,2,16]{1,3,2,0:T(8,128)S(1)} %get-tuple-element.271), channel_id=2, replica_groups=mesh['slot'=16,'head'=2,'conv'=4] {'slot'}, dimensions={0}, use_global_device_ids=true | all-gather | bytes 557056 | tf_op jit(solution)/shard_map/all_gather | solution.py:16
  134.5 0.9 copy-done.1
  135.4 13.9 %while.55 = (s32[]{:T(128)}, f32[4,64,2,16]{1,3,2,0:T(8,128)S(1)}, f32[4,64,2,16]{1,3,2,0:T(8,128)S(1)}, f32[16,4,64,2,16]{2,4,3,1,0:T(8,128)}, f32[16,4,64,2,16...) while((s32[]{:T(128)}, f32[4,64,2,16]{1,3,2,0:T(8,128)S(1)}, f32[4,64,2,16]{1,3,2,0:T(8,128)S(1)}, ...), condition=%wide.region_5.6_spmd, body=%wide.region_4.5_spmd.sunk | while | flops 49157 | bytes 196731 | solution.py:22
  139.1 0.9 fusion.88
  149.7 31.2 %while.56 = (s32[]{:T(128)}, f32[4,64,2,16]{3,1,2,0:T(8,128)}, pred[4,64,1024]{2,1,0:T(8,128)(4,1)S(1)}, bf16[4,64,2,16,128]{4,3,1,2,0:T(8,128)(2,1)}, bf16[1024...) while((s32[]{:T(128)}, f32[4,64,2,16]{3,1,2,0:T(8,128)}, ...), condition=%wide.region_8.9_spmd, body=%wide.region_6.8_spmd.sunk | while | flops 1086322688 | bytes 21397652 | solution.py:90
  149.7 2.4 fusion.93
  152.2 4.7 fusion.94
  157.6 2.4 fusion.93
  159.9 4.7 fusion.94
  165.4 2.4 fusion.93
  167.7 4.7 fusion.94
  173.1 2.4 fusion.93
  175.5 4.7 fusion.94
  180.9 61.1 %psum.28 = f32[4,64,2,16]{3,1,2,0:T(8,128)S(1)} all-reduce(f32[4,64,2,16]{3,1,2,0:T(8,128)} %get-tuple-element.275), channel_id=1, replica_groups=mesh['slot'=16,'head'=2,'conv'=4] {'slot'}, use_global_device_ids=true, to_apply=%region_9.10 | all-reduce | flops 8192 | bytes 65536 | tf_op jit(solution)/shard_map/psum | solution.py:91
  242.1 52.8 %while.57 = (s32[]{:T(128)}, f32[1024,2,128]{0,2,1:T(8,128)S(1)}, f32[1024,2,128]{0,2,1:T(8,128)S(1)}, f32[4,64,2,16,128]{4,3,2,1,0:T(8,128)}, bf16[4,64,2,16,12...) while((s32[]{:T(128)}, f32[1024,2,128]{0,2,1:T(8,128)S(1)}, ...), condition=%wide.region_11.12_spmd.clone, body=%wide.region_10.11_spmd.clone.sunk | while | flops 2711093248 | bytes 59867360 | solution.py:117
  242.1 2.4 fusion.105
  244.6 2.7 fusion.108
  247.3 3.5 fusion.106
  250.8 2.1 fusion.107
  252.9 1.2 fusion.109
  254.1 1.1 copy_dynamic-update-slice_fusion.2
  255.3 2.4 fusion.105
  257.8 2.7 fusion.108
  260.5 3.5 fusion.106
  263.9 2.1 fusion.107
  266.0 1.2 fusion.109
  267.3 1.2 copy_dynamic-update-slice_fusion.2
  268.5 2.4 fusion.105
  271.0 2.7 fusion.108
  273.7 3.5 fusion.106
  277.1 2.1 fusion.107
  279.2 1.2 fusion.109
  280.5 1.1 copy_dynamic-update-slice_fusion.2
  281.6 2.4 fusion.105
  284.1 2.7 fusion.108
  286.8 3.5 fusion.106
  290.3 2.1 fusion.107
  292.4 1.2 fusion.109
  293.6 1.2 copy_dynamic-update-slice_fusion.2
  294.8 1.3 copy.52
  296.1 1.3 copy.53
  298.1 81.6 %all-reduce.6.cloned.1.call-done = (f32[1,1024,2,128]{3,2,1,0:T(2,128)}, f32[1,1024,2,128]{3,2,1,0:T(2,128)}) async-done(((f32[1,1024,2,128]{3,2,1,0:T(2,128)}, f32[1,1024,2,128]{3,2,1,0:T(2,128)}), (f32[1,1024,2,128]{3,2,1,0:T(2,128)}, f32[1,1024,2,128]{3,2,1,0:T(2,128)})) %all-reduce.6.cloned.1.call-update) | async-done | bytes 2097168 | tf_op jit(solution)/shard_map/psum | solution.py:126
  379.7 1.3 constant_dynamic-update-slice_fusion.3
  381.0 1.4 constant_dynamic-update-slice_fusion.2
  382.4 9.8 %divide_subtract_fusion = (f32[2,1024,2,128]{3,2,1,0:T(2,128)}, f32[2,1024,2,128]{3,2,1,0:T(2,128)}, f32[2,1024,2,128]{3,2,1,0:T(2,128)}) fusion(f32[2,1024,2,128]{3,2,1,0:T(2,128)} %param.19, f32[2,1024,2,128]{3,2,1,0:T(2,128)S(1)} %constant_dynamic-update-slice_fusion.2, f32[2,1024,2,128]{3,2,1,0:T(2,128)} %param.20, f32[2,1024,2,128]{3,2,1,0:T(2,128)} %param.21), kind=kLoop, calls=%fused_computation.80 | loop fusion | flops 6291456 | bytes 14680064 | tf_op jit(solution)/shard_map/sub | solution.py:132
  392.2 93.3 %all-reduce.4.cloned.1.call-done = f32[256,32,128]{2,1,0:T(8,128)} async-done(((f32[256,32,128]{2,1,0:T(8,128)}), f32[256,32,128]{2,1,0:T(8,128)}) %all-reduce.4.cloned.1.call-update) | async-done | bytes 4194320 | tf_op jit(solution)/shard_map/psum | solution.py:123
  485.5 1.7 constant_dynamic-slice_fusion
  (101 shorter events, 19.1 us)
Async XLA Ops:
  7.2 12.3 %copy-start.6 = (s32[256]{0:T(256)S(1)}, s32[256]{0:T(256)}, u32[]{:S(2)}) copy-start(s32[256]{0:T(256)} %param.17) | copy-start | bytes 3076
  7.2 64.4 %all-gather.4.cloned.1.call-start = ((), (), s32[]{:S(2)}) async-start(), calls=%async_computation.1 | async-start | bytes 2228224 | tf_op jit(solution)/shard_map/all_gather | solution.py:43
  10.5 10.8 %copy-start.5 = (s32[1024]{0:T(1024)S(1)}, s32[1024]{0:T(1024)}, u32[]{:S(2)}) copy-start(s32[1024]{0:T(1024)} %param.18) | copy-start | bytes 12292
  10.5 39.1 %all-to-all-start = ((bf16[16,16,32,128]{3,2,1,0:T(8,128)(2,1)}), bf16[16,16,32,128]{3,2,1,0:T(8,128)(2,1)}, u32[]{:S(2)}, u32[]{:S(2)}) async-start(bf16[16,16,32,128]{3,2,1,0:T(8,128)(2,1)} %stack.8), calls=%async_computation | async-start | bytes 4194304 | tf_op jit(solution)/shard_map/all_to_all | solution.py:38
  19.3 360.4 %all-reduce.6.cloned.1.call-start = ((), (), s32[]{:S(2)}) async-start(), calls=%async_computation.3 | async-start | bytes 4194304 | tf_op jit(solution)/shard_map/psum | solution.py:126
  134.5 1.0 copy-start.1
  149.7 92.4 %copy-start.2 = (f32[1024,2,128]{0,2,1:T(8,128)S(1)}, f32[1024,2,128]{0,2,1:T(8,128)}, u32[]{:S(2)}) copy-start(f32[1024,2,128]{0,2,1:T(8,128)} %custom-call.1) | copy-start | bytes 3145732
  149.7 2.4 copy-start.3
  157.6 2.4 copy-start.3
  165.4 2.4 copy-start.3
  173.1 2.4 copy-start.3
  242.1 2.5 copy-start
  244.6 2.7 copy-start.4
  255.3 2.5 copy-start
  257.8 2.7 copy-start.4
  268.5 2.5 copy-start
  270.9 2.7 copy-start.4
  281.6 2.5 copy-start
  284.1 2.7 copy-start.4
  297.4 188.1 %all-reduce.4.cloned.1.call-start = ((), (), s32[]{:S(2)}) async-start(), calls=%async_computation.2 | async-start | bytes 8388608 | tf_op jit(solution)/shard_map/psum | solution.py:123
Sparse Core Ops, SparseCore 0:
  10.1 61.3 all-gather.3
  297.5 82.1 all-reduce.5
  383.1 102.3 all-reduce.3
